TPU v7x, 128 devices: a whole 4x4x4 slice. The times are simulated.
128 devices in a mesh: row: 8 (over x, y_hi), col: 16 (over y_lo, z, core).
Axes of the slice: x: 4, y: 4 (y_hi: 2, y_lo: 2; y = y_hi * 2 + y_lo), z: 4, core: 2. Of those that a mesh axis runs over, the one named last changes fastest.
Arguments:
- front_trailing: float32 [16384, 16384], P('row', 'col'), may hold values from -6 to 6
- panel_columns: float32 [16384, 1024], P('row', 'col'), may hold values from -0.1875 to 0.1875
- panel_rows: float32 [1024, 16384], P('row', 'col'), may hold values from -6 to 6
- pivots: int32 [1024], replicated, may hold values from 0 to 1023, each once
- diag_inverse: float32 [1024, 1024], replicated, may hold values from -0.1875 to 0.1875
- test_matrix: float32 [16384, 512], P('col'), may hold values from -0.046875 to 0.046875
Outputs:
- schur: float32 [16384, 16384], P('row', 'col')
- off_samples: float32 [16384, 512], P(('row', 'col'))
- leaf_blocks: float32 [16384, 128], P(('row', 'col'))
- group_gram: float32 [8, 512, 512], P('row')
Inputs may be any that keep to these rules, and one draw needn't show every extreme that they name: pivots names each of 0 to 1023 once.
All inputs are finite; a program needn't handle non-finite values.
Results may differ from a plain program's by a relative error of at most 0.000084.
Values sent between devices are 32-bit elements; how exact they have to be, the bound alone decides.
A program may use at most 128 MiB of HBM per device.

v0:
```python
import jax
import jax.numpy as jnp
from jax import lax
from jax.sharding import PartitionSpec as P

LEAF = 128


def product(left, right):
    return jnp.dot(left, right, precision=lax.Precision.HIGH, preferred_element_type=jnp.float32)


def body(front_trailing, panel_columns, panel_rows, pivots, diag_inverse, test_matrix):
    col_count = lax.axis_size("col")
    row_count = lax.axis_size("row")
    row_index = lax.axis_index("row")
    col_index = lax.axis_index("col")
    height, width = front_trailing.shape
    upper_full = lax.all_gather(panel_rows, "row", axis=0, tiled=True)
    left = lax.all_gather(panel_columns, "col", axis=1, tiled=True)
    upper = jnp.take(upper_full, pivots, axis=0)
    weight = product(diag_inverse, upper)
    schur = front_trailing - product(left, weight)
    rows = row_index * height + jnp.arange(height, dtype=jnp.int32)
    cols = col_index * width + jnp.arange(width, dtype=jnp.int32)
    same_leaf = rows[:, None] // LEAF == cols[None, :] // LEAF
    masked = jnp.where(same_leaf, jnp.zeros_like(schur), schur)
    partial = product(masked, test_matrix)
    count = width // LEAF
    ratio = col_count // row_count
    leaves = height // LEAF
    kept = []
    for leaf in range(leaves):
        held = col_index == row_index * ratio + leaf // count
        block = schur[
            leaf * LEAF : (leaf + 1) * LEAF, leaf % count * LEAF : (leaf % count + 1) * LEAF
        ]
        kept.append(jnp.where(held, block, jnp.zeros_like(block)))
    both = jnp.concatenate([partial, jnp.concatenate(kept, axis=0)], axis=1)
    own = lax.psum_scatter(both, "col", scatter_dimension=0, tiled=True)
    own_samples = own[:, : partial.shape[1]]
    leaf_blocks = own[:, partial.shape[1] :]
    gram = lax.dot_general(
        own_samples,
        own_samples,
        (((0,), (0,)), ((), ())),
        precision=lax.Precision.HIGH,
        preferred_element_type=jnp.float32,
    )
    gram = lax.psum(gram, "col")
    route = [(i, i ^ 1) for i in range(row_count)]
    gram = gram + lax.ppermute(gram, "row", route)
    group_gram = (gram / (2 * height))[None]
    return (schur, own_samples, leaf_blocks, group_gram)


def solution(mesh):
    placed = (P("row", "col"), P("row", "col"), P("row", "col"), P(), P(), P("col", None))
    return jax.shard_map(
        body,
        mesh=mesh,
        in_specs=placed,
        out_specs=(
            P("row", "col"),
            P(("row", "col"), None),
            P(("row", "col"), None),
            P("row", None, None),
        ),
        check_vma=False,
    )
```

profile of v0, /device:TPU:0, one launch (start us, length us, event | category | flops | bytes accessed | tf_op | source)
XLA Modules:
  0.0 392.7 jit_solution(6487991175751841340)
XLA Ops:
  7.2 0.0 copy-start
  7.2 0.0 all-gather.3.cloned.1.call-start
  7.2 0.7 all-gather.3.cloned.1.call-update
  7.9 0.0 all-gather.5.cloned.1.call-start
  8.0 0.7 all-gather.5.cloned.1.call-update
  8.7 0.0 reduce-scatter.2.cloned.1.call-start
  8.7 0.0 copy-start.3
  8.7 9.1 %copy.10 = f32[2048,1024]{0,1:T(8,128)} copy(f32[2048,1024]{1,0:T(8,128)} %param.6) | data formatting | bytes 16777216 | tf_op args[0]
  17.9 0.0 copy-done.3
  17.9 66.5 %all-gather.3.cloned.1.call-done = f32[1024,1024]{1,0:T(8,128)} async-done(((f32[128,1024]{1,0:T(8,128)}), f32[1024,1024]{1,0:T(8,128)}) %all-gather.3.cloned.1.call-update) | async-done | bytes 4194320 | tf_op jit(solution)/shard_map/all_gather | solution.py:19
  84.4 8.6 %gather_fusion = f32[1024,1024]{1,0:T(8,128)} fusion(f32[1024,1024]{1,0:T(8,128)} %all-gather.3.cloned.1.call-done, s32[1024]{0:T(1024)S(1)} %fusion.32), kind=kCustom, calls=%fused_computation | custom fusion | bytes 8392704 | tf_op jit(solution)/shard_map/jit(_take)/gather | solution.py:21
  93.0 17.9 %fusion.5 = f32[1024,1024]{1,0:T(8,128)} fusion(f32[1024,1024]{1,0:T(8,128)} %param.10, f32[1024,1024]{1,0:T(8,128)} %gather_fusion, pred[1024]{0:T(1024)(128)(4,1)S(1)} %compare_and_fusion), kind=kOutput, calls=%fused_computation.8 | convolution fusion | flops 6443499520 | bytes 12583936 | tf_op jit(solution)/shard_map/dot_general | solution.py:10
  110.9 25.2 %all-gather.5.cloned.1.call-done = f32[2048,1024]{0,1:T(8,128)} async-done(((f32[2048,64]{0,1:T(8,128)}), f32[2048,1024]{0,1:T(8,128)}) %all-gather.5.cloned.1.call-update) | async-done | bytes 8388624 | tf_op jit(solution)/shard_map/all_gather | solution.py:20
  136.1 17.8 %bitcast_subtract_fusion = f32[2048,1024]{0,1:T(8,128)S(1)} fusion(f32[2048,1024]{0,1:T(8,128)} %copy.10, f32[1024,1024]{1,0:T(8,128)} %fusion.5, f32[2048,1024]{0,1:T(8,128)} %all-gather.5.cloned.1.call-done), kind=kOutput, calls=%fused_computation.1 | convolution fusion | flops 12886999040 | bytes 29360128 | tf_op jit(solution)/shard_map/dot_general | solution.py:10
  154.0 0.0 copy-start.1
  154.3 0.0 copy-done
  154.3 7.6 %fusion = f32[2048,512]{0,1:T(8,128)S(1)} fusion(f32[1024,512]{1,0:T(8,128)S(1)} %copy-done, f32[2048,1024]{0,1:T(8,128)S(1)} %bitcast_subtract_fusion, s32[2048]{0:T(1024)S(1)} %add_select_fusion, s32[1024]{0:T(1024)S(1)} %add_select_fusion.1), kind=kOutput, calls=%fused_computation.2 | convolution fusion | flops 6446645248 | bytes 14692352 | tf_op jit(solution)/shard_map/dot_general | solution.py:10
  161.9 0.0 copy-done.1
  161.9 3.0 pad_maximum_fusion
  164.9 0.0 reduce-scatter.2.cloned.1.call-update
  164.9 0.0 all-reduce.2.cloned.1.call-start
  165.0 70.5 %reduce-scatter.2.cloned.1.call-done = f32[128,640]{0,1:T(8,128)} async-done(((f32[2048,640]{0,1:T(8,128)}), f32[128,640]{0,1:T(8,128)}) %reduce-scatter.2.cloned.1.call-update) | async-done | bytes 327696 | tf_op jit(solution)/shard_map/reduce_scatter | solution.py:40
  235.5 2.6 fusion.35
  238.1 0.0 all-reduce.2.cloned.1.call-update
  238.1 0.0 slice-start
  238.1 0.0 slice-start.1
  238.1 119.0 %all-reduce.2.cloned.1.call-done = f32[512,512]{1,0:T(8,128)} async-done(((f32[512,512]{1,0:T(8,128)}), f32[512,512]{1,0:T(8,128)}) %all-reduce.2.cloned.1.call-update) | async-done | bytes 1048592 | tf_op jit(solution)/shard_map/psum | solution.py:50
  357.1 0.0 copy-start.2
  357.1 2.7 collective-permute-start
  359.8 9.2 %copy.11 = f32[2048,1024]{1,0:T(8,128)} copy(f32[2048,1024]{0,1:T(8,128)} %copy-done.1) | data formatting | bytes 16777216
  369.1 0.0 slice-done
  369.1 0.8 copy.12
  369.9 0.0 slice-done.1
  369.9 0.7 copy.13
  370.6 13.1 %collective-permute-done = f32[512,512]{1,0:T(8,128)} collective-permute-done((f32[512,512]{1,0:T(8,128)}, f32[512,512]{1,0:T(8,128)}, u32[]{:S(2)}, u32[]{:S(2)}) %collective-permute-start) | collective-permute-done | bytes 1048608 | tf_op jit(solution)/shard_map/ppermute | solution.py:52
  383.7 0.0 copy-done.2
  383.7 2.4 multiply_bitcast_fusion
  (20 shorter events, 0.2 us)
Async XLA Ops:
  7.2 147.1 %copy-start = (f32[1024,512]{1,0:T(8,128)S(1)}, f32[1024,512]{1,0:T(8,128)}, u32[]{:S(2)}) copy-start(f32[1024,512]{1,0:T(8,128)} %param.11) | copy-start | bytes 6291460
  7.2 77.2 %all-gather.3.cloned.1.call-start = ((), (), s32[]{:S(2)}) async-start(), calls=%async_computation.1 | async-start | bytes 4718592 | tf_op jit(solution)/shard_map/all_gather | solution.py:19
  7.9 128.2 %all-gather.5.cloned.1.call-start = ((), (), s32[]{:S(2)}) async-start(), calls=%async_computation.2 | async-start | bytes 8912896 | tf_op jit(solution)/shard_map/all_gather | solution.py:20
  8.7 226.8 %reduce-scatter.2.cloned.1.call-start = ((), (), s32[]{:S(2)}) async-start(), calls=%async_computation.3 | async-start | bytes 5570560 | tf_op jit(solution)/shard_map/reduce_scatter | solution.py:40
  8.7 9.2 %copy-start.3 = (s32[1024]{0:T(1024)S(1)}, s32[1024]{0:T(1024)}, u32[]{:S(2)}) copy-start(s32[1024]{0:T(1024)} %param.9) | copy-start | bytes 12292
  154.0 7.9 %copy-start.1 = (f32[2048,1024]{0,1:T(8,128)}, f32[2048,1024]{0,1:T(8,128)S(1)}, u32[]{:S(2)}) copy-start(f32[2048,1024]{0,1:T(8,128)S(1)} %bitcast_subtract_fusion) | copy-start | bytes 25165828
  164.9 192.2 %all-reduce.2.cloned.1.call-start = ((), (), s32[]{:S(2)}) async-start(), calls=%async_computation.4 | async-start | bytes 2097152 | tf_op jit(solution)/shard_map/psum | solution.py:50
  238.1 131.0 %slice-start = ((f32[128,640]{0,1:T(8,128)}), f32[128,512]{0,1:T(8,128)S(1)}, s32[]{:S(2)}) async-start(f32[128,640]{0,1:T(8,128)} %reduce-scatter.2.cloned.1.call-done), calls=%async_computation.5 | async-start | bytes 524288 | tf_op jit(solution)/shard_map/slice | solution.py:41
  238.1 131.8 %slice-start.1 = ((f32[128,640]{0,1:T(8,128)}), f32[128,128]{0,1:T(8,128)S(1)}, s32[]{:S(2)}) async-start(f32[128,640]{0,1:T(8,128)} %reduce-scatter.2.cloned.1.call-done), calls=%async_computation.6 | async-start | bytes 131072 | tf_op jit(solution)/shard_map/slice | solution.py:42
  357.1 26.6 %copy-start.2 = (f32[512,512]{1,0:T(8,128)S(1)}, f32[512,512]{1,0:T(8,128)}, u32[]{:S(2)}) copy-start(f32[512,512]{1,0:T(8,128)} %all-reduce.2.cloned.1.call-done) | copy-start | bytes 3145732
  357.1 26.6 %collective-permute-start = (f32[512,512]{1,0:T(8,128)}, f32[512,512]{1,0:T(8,128)}, u32[]{:S(2)}, u32[]{:S(2)}) collective-permute-start(f32[512,512]{1,0:T(8,128)} %all-reduce.2.cloned.1.call-done), channel_id=1, source_target_pairs={{0,16},{16,0},{32,48},{48,32},{64,80},{80,64},{96,112},{112,96},{1... | collective-permute-start | bytes 3145736 | tf_op jit(solution)/shard_map/ppermute | solution.py:52
Sparse Core Ops, SparseCore 0:
  10.3 74.0 all-gather.2
  86.1 49.9 all-gather.4
  165.0 70.3 reduce-scatter.1
  238.4 118.7 all-reduce.1
where the time goes:
time: 393 us
  waiting for transfers between devices  296 us (75%)
  matrix products  45.9 us (12%)
  local copies, waits for them, and re-layouts  28.6 us (7%)
  between operations  14 us (4%)
  other arithmetic  5.64 us (1%)
    psum x1, waiting for transfers between devices, body(): gram = lax.psum(gram, 'col')  119 us
    reduce_scatter x1, waiting for transfers between devices, body(): own = lax.psum_scatter(both, 'col', scatter_dimension=0, tiled=True)  70.5 us
    all_gather x1, waiting for transfers between devices, body(): upper_full = lax.all_gather(panel_rows, 'row', axis=0, tiled=True)  66.5 us
    dot_general x3, matrix products, product(): jnp.dot(left, right, precision=lax.Precision.HIGH, preferred_element_type...  43.3 us
    all_gather x1, waiting for transfers between devices, body(): left = lax.all_gather(panel_columns, 'col', axis=1, tiled=True)  25.2 us
    unnamed x12, local copies, waits for them, and re-layouts  20 us
    ppermute x1, waiting for transfers between devices, body(): gram = gram + lax.ppermute(gram, 'row', route)  13.1 us
    gather x1, local copies, waits for them, and re-layouts, body(): upper = jnp.take(upper_full, pivots, axis=0)  8.63 us
  transfers between devices with their start and end apart: 5, of which 5 were waited for; matrix products, arithmetic and copies ran while one was open for 12% of the time, Pallas kernels for 0%

commit v1 on v0

--- a/solution.py
+++ b/solution.py
@@ -17,7 +17,9 @@
     col_index = lax.axis_index("col")
     height, width = front_trailing.shape
     upper_full = lax.all_gather(panel_rows, "row", axis=0, tiled=True)
-    left = lax.all_gather(panel_columns, "col", axis=1, tiled=True)
+    left = jnp.concatenate(
+        lax.all_to_all(jnp.stack([panel_columns] * lax.axis_size("col")), "col", 0, 0), axis=1
+    )
     upper = jnp.take(upper_full, pivots, axis=0)
     weight = product(diag_inverse, upper)
     schur = front_trailing - product(left, weight)

time: 393 us -> 415 us (1.056)
  waiting for transfers between devices: 296 us -> 306 us
  starting transfers between devices: 2.88 us -> 9.43 us
  local copies, waits for them, and re-layouts: 28.6 us -> 34 us
    all_gather x1 -> x0, waiting for transfers between devices: 25.2 us -> none  [body(): left = lax.all_gather(panel_columns, 'col', axis=1, tiled=True)]
    all_gather x1, waiting for transfers between devices: 66.5 us -> 82.3 us  [body(): upper_full = lax.all_gather(panel_rows, 'row', axis=0, tiled=True)]
    all_to_all x0 -> x1, waiting for transfers between devices: none -> 12.9 us  [body(): lax.all_to_all(jnp.stack([panel_columns] * lax.axis_size('col')), 'col',...]
    reduce_scatter x1, waiting for transfers between devices: 70.5 us -> 77.6 us  [body(): own = lax.psum_scatter(both, 'col', scatter_dimension=0, tiled=True)]
    all_to_all x0 -> x1, starting transfers between devices: none -> 6.59 us  [body(): lax.all_to_all(jnp.stack([panel_columns] * lax.axis_size('col')), 'col',...]
    another operation x0 -> x1, local copies, waits for them, and re-layouts: none -> 5.36 us  [body(): jnp.stack([panel_columns] * lax.axis_size('col'))]
where the time goes in v1:
time: 415 us
  waiting for transfers between devices  306 us (74%)
  matrix products  45.8 us (11%)
  local copies, waits for them, and re-layouts  34 us (8%)
  between operations  14 us (3%)
  starting transfers between devices  9.43 us (2%)
  other arithmetic  5.64 us (1%)
    psum x1, waiting for transfers between devices, body(): gram = lax.psum(gram, 'col')  119 us
    all_gather x1, waiting for transfers between devices, body(): upper_full = lax.all_gather(panel_rows, 'row', axis=0, tiled=True)  82.3 us
    reduce_scatter x1, waiting for transfers between devices, body(): own = lax.psum_scatter(both, 'col', scatter_dimension=0, tiled=True)  77.6 us
    dot_general x3, matrix products, product(): jnp.dot(left, right, precision=lax.Precision.HIGH, preferred_element_type...  43.2 us
    unnamed x12, local copies, waits for them, and re-layouts  20 us
    ppermute x1, waiting for transfers between devices, body(): gram = gram + lax.ppermute(gram, 'row', route)  13.1 us
    all_to_all x1, waiting for transfers between devices, body(): lax.all_to_all(jnp.stack([panel_columns] * lax.axis_size('col')), 'col',...  12.9 us
    gather x1, local copies, waits for them, and re-layouts, body(): upper = jnp.take(upper_full, pivots, axis=0)  8.6 us
  transfers between devices with their start and end apart: 5, of which 5 were waited for; matrix products, arithmetic and copies ran while one was open for 12% of the time, Pallas kernels for 0%

profile of v1, /device:TPU:0, one launch (start us, length us, event | category | flops | bytes accessed | tf_op | source)
XLA Modules:
  0.0 414.5 jit_solution(6842408788366659100)
XLA Ops:
  7.2 0.0 copy-start
  7.2 0.0 all-gather.2.cloned.1.call-start
  7.2 0.7 all-gather.2.cloned.1.call-update
  7.9 5.4 %stack.2 = f32[16,2048,64]{1,2,0:T(8,128)} broadcast(f32[2048,64]{0,1:T(8,128)} %param.7), dimensions={1,2} | broadcast | bytes 8912896 | tf_op jit(solution)/shard_map/stack | solution.py:21
  13.3 6.6 %all-to-all-start = ((f32[16,2048,64]{1,2,0:T(8,128)}), f32[16,2048,64]{1,2,0:T(8,128)}, u32[]{:S(2)}, u32[]{:S(2)}) async-start(f32[16,2048,64]{1,2,0:T(8,128)} %stack.2), calls=%async_computation | async-start | bytes 16777216 | tf_op jit(solution)/shard_map/all_to_all | solution.py:21
  19.9 0.0 reduce-scatter.2.cloned.1.call-start
  19.9 0.0 copy-start.3
  19.9 9.2 %copy.15 = f32[2048,1024]{0,1:T(8,128)} copy(f32[2048,1024]{1,0:T(8,128)} %param.6) | data formatting | bytes 16777216 | tf_op args[0]
  29.2 0.0 copy-done.3
  29.2 82.3 %all-gather.2.cloned.1.call-done = f32[1024,1024]{1,0:T(8,128)} async-done(((f32[128,1024]{1,0:T(8,128)}), f32[1024,1024]{1,0:T(8,128)}) %all-gather.2.cloned.1.call-update) | async-done | bytes 4194320 | tf_op jit(solution)/shard_map/all_gather | solution.py:19
  111.4 8.6 %gather_fusion = f32[1024,1024]{1,0:T(8,128)} fusion(f32[1024,1024]{1,0:T(8,128)} %all-gather.2.cloned.1.call-done, s32[1024]{0:T(1024)S(1)} %fusion.32), kind=kCustom, calls=%fused_computation | custom fusion | bytes 8392704 | tf_op jit(solution)/shard_map/jit(_take)/gather | solution.py:23
  120.1 17.8 %fusion.5 = f32[1024,1024]{1,0:T(8,128)} fusion(f32[1024,1024]{1,0:T(8,128)} %param.10, f32[1024,1024]{1,0:T(8,128)} %gather_fusion, pred[1024]{0:T(1024)(128)(4,1)S(1)} %compare_and_fusion), kind=kOutput, calls=%fused_computation.8 | convolution fusion | flops 6443499520 | bytes 12583936 | tf_op jit(solution)/shard_map/dot_general | solution.py:10
  137.9 12.9 %all-to-all-done = f32[16,2048,64]{1,2,0:T(8,128)} async-done(((f32[16,2048,64]{1,2,0:T(8,128)}), f32[16,2048,64]{1,2,0:T(8,128)}, u32[]{:S(2)}, u32[]{:S(2)}) %all-to-all-start) | async-done | bytes 8388640 | tf_op jit(solution)/shard_map/all_to_all | solution.py:21
  150.7 17.8 %bitcast_subtract_fusion = f32[2048,1024]{0,1:T(8,128)S(1)} fusion(f32[2048,1024]{0,1:T(8,128)} %copy.15, f32[1024,1024]{1,0:T(8,128)} %fusion.5, f32[2048,1024]{0,1:T(8,128)} %bitcast.1), kind=kOutput, calls=%fused_computation.1 | convolution fusion | flops 12886999040 | bytes 29360128 | tf_op jit(solution)/shard_map/dot_general | solution.py:10
  168.6 0.0 copy-start.1
  168.9 0.0 copy-done
  168.9 7.6 %fusion = f32[2048,512]{0,1:T(8,128)S(1)} fusion(f32[1024,512]{1,0:T(8,128)S(1)} %copy-done, f32[2048,1024]{0,1:T(8,128)S(1)} %bitcast_subtract_fusion, s32[2048]{0:T(1024)S(1)} %add_select_fusion, s32[1024]{0:T(1024)S(1)} %add_select_fusion.1), kind=kOutput, calls=%fused_computation.2 | convolution fusion | flops 6446645248 | bytes 14692352 | tf_op jit(solution)/shard_map/dot_general | solution.py:10
  176.5 0.0 copy-done.1
  176.5 3.0 pad_maximum_fusion
  179.5 0.0 reduce-scatter.2.cloned.1.call-update
  179.5 0.0 all-reduce.2.cloned.1.call-start
  179.6 77.6 %reduce-scatter.2.cloned.1.call-done = f32[128,640]{0,1:T(8,128)} async-done(((f32[2048,640]{0,1:T(8,128)}), f32[128,640]{0,1:T(8,128)}) %reduce-scatter.2.cloned.1.call-update) | async-done | bytes 327696 | tf_op jit(solution)/shard_map/reduce_scatter | solution.py:42
  257.1 2.6 fusion.35
  259.8 0.0 all-reduce.2.cloned.1.call-update
  259.8 0.0 slice-start
  259.8 0.0 slice-start.1
  259.8 119.1 %all-reduce.2.cloned.1.call-done = f32[512,512]{1,0:T(8,128)} async-done(((f32[512,512]{1,0:T(8,128)}), f32[512,512]{1,0:T(8,128)}) %all-reduce.2.cloned.1.call-update) | async-done | bytes 1048592 | tf_op jit(solution)/shard_map/psum | solution.py:52
  379.0 0.0 copy-start.2
  379.0 2.7 collective-permute-start
  381.7 9.2 %copy.16 = f32[2048,1024]{1,0:T(8,128)} copy(f32[2048,1024]{0,1:T(8,128)} %copy-done.1) | data formatting | bytes 16777216
  390.9 0.0 slice-done
  390.9 0.8 copy.17
  391.8 0.0 slice-done.1
  391.8 0.7 copy.18
  392.5 13.1 %collective-permute-done = f32[512,512]{1,0:T(8,128)} collective-permute-done((f32[512,512]{1,0:T(8,128)}, f32[512,512]{1,0:T(8,128)}, u32[]{:S(2)}, u32[]{:S(2)}) %collective-permute-start) | collective-permute-done | bytes 1048608 | tf_op jit(solution)/shard_map/ppermute | solution.py:54
  405.6 0.0 copy-done.2
  405.6 2.4 multiply_bitcast_fusion
  (20 shorter events, 0.2 us)
Async XLA Ops:
  7.2 161.7 %copy-start = (f32[1024,512]{1,0:T(8,128)S(1)}, f32[1024,512]{1,0:T(8,128)}, u32[]{:S(2)}) copy-start(f32[1024,512]{1,0:T(8,128)} %param.11) | copy-start | bytes 6291460
  7.2 104.3 %all-gather.2.cloned.1.call-start = ((), (), s32[]{:S(2)}) async-start(), calls=%async_computation.2 | async-start | bytes 4718592 | tf_op jit(solution)/shard_map/all_gather | solution.py:19
  13.3 137.5 %all-to-all-start = ((f32[16,2048,64]{1,2,0:T(8,128)}), f32[16,2048,64]{1,2,0:T(8,128)}, u32[]{:S(2)}, u32[]{:S(2)}) async-start(f32[16,2048,64]{1,2,0:T(8,128)} %stack.2), calls=%async_computation | async-start | bytes 16777216 | tf_op jit(solution)/shard_map/all_to_all | solution.py:21
  19.9 237.3 %reduce-scatter.2.cloned.1.call-start = ((), (), s32[]{:S(2)}) async-start(), calls=%async_computation.3 | async-start | bytes 5570560 | tf_op jit(solution)/shard_map/reduce_scatter | solution.py:42
  19.9 9.2 %copy-start.3 = (s32[1024]{0:T(1024)S(1)}, s32[1024]{0:T(1024)}, u32[]{:S(2)}) copy-start(s32[1024]{0:T(1024)} %param.9) | copy-start | bytes 12292
  168.6 7.9 %copy-start.1 = (f32[2048,1024]{0,1:T(8,128)}, f32[2048,1024]{0,1:T(8,128)S(1)}, u32[]{:S(2)}) copy-start(f32[2048,1024]{0,1:T(8,128)S(1)} %bitcast_subtract_fusion) | copy-start | bytes 25165828
  179.5 199.4 %all-reduce.2.cloned.1.call-start = ((), (), s32[]{:S(2)}) async-start(), calls=%async_computation.4 | async-start | bytes 2097152 | tf_op jit(solution)/shard_map/psum | solution.py:52
  259.8 131.1 %slice-start = ((f32[128,640]{0,1:T(8,128)}), f32[128,512]{0,1:T(8,128)S(1)}, s32[]{:S(2)}) async-start(f32[128,640]{0,1:T(8,128)} %reduce-scatter.2.cloned.1.call-done), calls=%async_computation.5 | async-start | bytes 524288 | tf_op jit(solution)/shard_map/slice | solution.py:43
  259.8 132.0 %slice-start.1 = ((f32[128,640]{0,1:T(8,128)}), f32[128,128]{0,1:T(8,128)S(1)}, s32[]{:S(2)}) async-start(f32[128,640]{0,1:T(8,128)} %reduce-scatter.2.cloned.1.call-done), calls=%async_computation.6 | async-start | bytes 131072 | tf_op jit(solution)/shard_map/slice | solution.py:44
  379.0 26.6 %copy-start.2 = (f32[512,512]{1,0:T(8,128)S(1)}, f32[512,512]{1,0:T(8,128)}, u32[]{:S(2)}) copy-start(f32[512,512]{1,0:T(8,128)} %all-reduce.2.cloned.1.call-done) | copy-start | bytes 3145732
  379.0 26.6 %collective-permute-start = (f32[512,512]{1,0:T(8,128)}, f32[512,512]{1,0:T(8,128)}, u32[]{:S(2)}, u32[]{:S(2)}) collective-permute-start(f32[512,512]{1,0:T(8,128)} %all-reduce.2.cloned.1.call-done), channel_id=1, source_target_pairs={{0,16},{16,0},{32,48},{48,32},{64,80},{80,64},{96,112},{112,96},{1... | collective-permute-start | bytes 3145736 | tf_op jit(solution)/shard_map/ppermute | solution.py:54
Sparse Core Ops, SparseCore 0:
  10.3 101.0 all-gather.1
  179.6 77.4 reduce-scatter.1
  260.2 118.7 all-reduce.1
